TPU v7x, 256 devices: a whole 4x4x8 slice. The times are simulated.
256 devices in a mesh: seq: 16 (over y, x), fsdp: 16 (over z, core).
Axes of the slice: x: 4, y: 4, z: 8, core: 2. Of those that a mesh axis runs over, the one named last changes fastest.
Arguments:
- kv_cache: bfloat16 [2, 32, 8192, 1280], P(None, 'fsdp', 'seq'), may hold values from -6 to 6
- keep_flags: int32 [32, 8192], P('fsdp', 'seq'), may hold values from 0 to 1, as said below
- block_weights: float32 [32, 8192], P('fsdp', 'seq'), may hold values from 0.05 to 2
- lengths: int32 [32], P('fsdp'), may hold values from 2048 to 8192, as said below
- token_qkv: bfloat16 [32, 3840], P('fsdp'), may hold values from -10 to 10
- stream: bfloat16 [32, 1280], P('fsdp'), may hold values from -0.59765625 to 0.59765625
- w_out: bfloat16 [1280, 1280], P(None, 'fsdp'), may hold values from -0.15625 to 0.15625
- w_up: bfloat16 [1280, 1280], P(None, 'fsdp'), may hold values from -0.15625 to 0.15625
- w_down: bfloat16 [1280, 1280], P(None, 'fsdp'), may hold values from -0.15625 to 0.15625
- w_qkv: bfloat16 [1280, 3840], P(None, 'fsdp'), may hold values from -0.15625 to 0.15625
- mlp_gain: float32 [1280], replicated, may hold values from 0.1 to 1.9
- next_gain: float32 [1280], replicated, may hold values from 0.1 to 1.9
Outputs:
- packed_cache: bfloat16 [2, 32, 8192, 1280], P(None, 'fsdp', 'seq')
- block_summary: bfloat16 [2, 32, 512, 1280], P(None, 'fsdp', 'seq')
- layer_out: bfloat16 [32, 1280], P('fsdp', 'seq')
- next_qkv: bfloat16 [32, 3840], P('fsdp', 'seq')
Inputs may be any that keep to these rules, and one draw needn't show every extreme that they name: `keep_flags`: in every draw one request keeps all 512 positions of one aligned block of 512 positions. `lengths`: in every draw some request has 8192 filled positions.
All inputs are finite; a program needn't handle non-finite values.
Results may differ from a plain program's by a relative error of at most 0.02.
Values may be sent and summed in bfloat16 or wider, within the bound.
A program may use at most 128 MiB of HBM per device.

v0:
```python
import math
import jax
import jax.numpy as jnp
from jax import lax
from jax.sharding import PartitionSpec as P

H = 16
BLK = 16
neg_fill = -1e30


def combined_all(part, axis, combine):
    gathered = jax.tree.map(lambda a: lax.all_gather(a, axis), part)

    def take(source):
        return jax.tree.map(lambda a: lax.dynamic_index_in_dim(a, source, 0, False), gathered)

    return lax.fori_loop(
        1, lax.axis_size(axis), lambda source, state: combine(state, take(source)), take(0)
    )


def normalize(values, gain):
    wide = values.astype(jnp.float32)
    factor = lax.rsqrt(jnp.mean(wide * wide, axis=-1, keepdims=True) + 1e-06)
    return (wide * factor * gain).astype(jnp.bfloat16)


def combine_parts(first, second):
    peak_a, total_a, accum_a = first
    peak_b, total_b, accum_b = second
    peak = jnp.maximum(peak_a, peak_b)
    factor_a = jnp.exp(peak_a - peak)
    factor_b = jnp.exp(peak_b - peak)
    return (
        peak,
        total_a * factor_a + total_b * factor_b,
        accum_a * factor_a[..., None] + accum_b * factor_b[..., None],
    )


def partial_softmax(queries, keys, values, usable, inv_root):
    scores = (
        jnp.einsum("rhe,rnhe->rhn", queries, keys, preferred_element_type=jnp.float32) * inv_root
    )
    scores = jnp.where(usable[:, None, :], scores, neg_fill)
    peak = jnp.max(scores, axis=-1)
    expo = jnp.where(usable[:, None, :], jnp.exp(scores - peak[..., None]), 0.0)
    total = jnp.sum(expo, axis=-1)
    accum = jnp.einsum("rhn,rnhe->rhe", expo, values, preferred_element_type=jnp.float32)
    return (peak, total, accum)


def split_heads(block):
    return block.reshape(block.shape[:-1] + (H, block.shape[-1] // H))


def body(
    kv_cache,
    keep_flags,
    block_weights,
    lengths,
    token_qkv,
    stream,
    w_out,
    w_up,
    w_down,
    w_qkv,
    mlp_gain,
    next_gain,
):
    seq_count = lax.axis_size("seq")
    seq_here = lax.axis_index("seq")
    reqs = kv_cache.shape[1]
    rows = kv_cache.shape[2]
    width = kv_cache.shape[3]
    head_size = width // H
    inv_root = 1.0 / math.sqrt(head_size)
    position = seq_here * rows + jnp.arange(rows, dtype=jnp.int32)
    in_range = position[None, :] < lengths[:, None]
    kept_rows = in_range & (keep_flags == 1)
    drop_rows = in_range & (keep_flags == 0)
    inclusive = jnp.cumsum(kept_rows.astype(jnp.int32), axis=1)
    held = inclusive[:, -1]
    every = lax.all_gather(held[None, :], "seq", axis=0, tiled=True)
    lower = jnp.arange(seq_count, dtype=jnp.int32)[:, None] < seq_here
    before = jnp.sum(jnp.where(lower, every, 0), axis=0)
    blocks = rows // BLK
    drop_weight = jnp.where(drop_rows, block_weights, 0.0).reshape(reqs, blocks, BLK)
    weight_total = jnp.sum(drop_weight, axis=-1)
    drop_count = jnp.sum(drop_rows.reshape(reqs, blocks, BLK).astype(jnp.int32), axis=-1)
    sums = jnp.einsum(
        "rbk,crbkd->crbd",
        drop_weight,
        kv_cache.reshape(2, reqs, blocks, BLK, width),
        preferred_element_type=jnp.float32,
        precision=lax.Precision.HIGHEST,
    )
    block_summary = (sums / jnp.maximum(weight_total, 1.0)[None, :, :, None]).astype(jnp.bfloat16)
    queries = split_heads(token_qkv[:, :width])
    own_keys = split_heads(token_qkv[:, width : 2 * width])
    own_values = split_heads(token_qkv[:, 2 * width :])
    slot = rows // seq_count
    target = jnp.arange(seq_count, dtype=jnp.int32)
    offset = jnp.mod(target[:, None] - before[None, :], seq_count)
    sent = (held[None, :] - offset + seq_count - 1) // seq_count
    wanted = offset[:, :, None] + seq_count * jnp.arange(slot, dtype=jnp.int32)[None, None, :]
    local_rank = inclusive - 1
    wanted_r = jnp.transpose(wanted, (1, 0, 2))
    pick_send = (
        kept_rows[:, None, None, :] & (local_rank[:, None, None, :] == wanted_r[:, :, :, None])
    ).astype(jnp.bfloat16)
    outgoing = jnp.einsum(
        "rtsp,crpd->ctrsd", pick_send, kv_cache, preferred_element_type=jnp.float32
    ).astype(jnp.bfloat16)
    incoming, arrived = (
        lax.all_to_all(outgoing, "seq", split_axis=1, concat_axis=1, tiled=True),
        lax.all_to_all(sent[None], "seq", split_axis=1, concat_axis=1, tiled=True),
    )
    counts_in = arrived[0]
    ends = jnp.cumsum(counts_in, axis=0)
    starts = ends - counts_in
    filled = ends[-1]
    local_rows = jnp.arange(rows, dtype=jnp.int32)
    slot_index = jnp.arange(slot, dtype=jnp.int32)
    starts_r = starts.T
    counts_r = counts_in.T
    valid_slot = slot_index[None, None, :] < counts_r[:, :, None]
    dest_row = starts_r[:, :, None] + slot_index[None, None, :]
    pick_recv = (
        valid_slot[:, None, :, :] & (dest_row[:, None, :, :] == local_rows[None, :, None, None])
    ).astype(jnp.bfloat16)
    packed_cache = jnp.einsum(
        "rlts,ctrsd->crld", pick_recv, incoming, preferred_element_type=jnp.float32
    ).astype(jnp.bfloat16)
    present = local_rows[None, :] < filled[:, None]
    row_part = partial_softmax(
        queries, split_heads(packed_cache[0]), split_heads(packed_cache[1]), present, inv_root
    )
    summary_part = partial_softmax(
        queries,
        split_heads(block_summary[0]),
        split_heads(block_summary[1]),
        drop_count > 0,
        inv_root,
    )
    peak, total, accum = combined_all(combine_parts(row_part, summary_part), "seq", combine_parts)
    own_score = (
        jnp.einsum("rhe,rhe->rh", queries, own_keys, preferred_element_type=jnp.float32) * inv_root
    )
    top_score = jnp.maximum(peak, own_score)
    factor_old = jnp.exp(peak - top_score)
    factor_own = jnp.exp(own_score - top_score)
    attended = (
        accum * factor_old[..., None] + factor_own[..., None] * own_values.astype(jnp.float32)
    ) / (total * factor_old + factor_own)[..., None]
    attended = attended.reshape(reqs, width).astype(jnp.bfloat16)
    fsdp_here = lax.axis_index("fsdp")

    def widen(columns):
        return lax.all_gather(columns, "fsdp", axis=1, tiled=True)

    def own_columns(full, count):
        return lax.dynamic_slice_in_dim(full, fsdp_here * count, count, 1)

    attn_all, stream_all = (
        lax.all_gather(attended, "fsdp", axis=0, tiled=True),
        lax.all_gather(stream, "fsdp", axis=0, tiled=True),
    )
    mid_cols = own_columns(stream_all, w_out.shape[1]).astype(jnp.float32) + jnp.dot(
        attn_all, w_out, preferred_element_type=jnp.float32
    )
    mid = widen(mid_cols.astype(jnp.bfloat16))
    hidden = widen(
        jax.nn.silu(
            jnp.dot(normalize(mid, mlp_gain), w_up, preferred_element_type=jnp.float32)
        ).astype(jnp.bfloat16)
    )
    out_cols = own_columns(mid, w_down.shape[1]).astype(jnp.float32) + jnp.dot(
        hidden, w_down, preferred_element_type=jnp.float32
    )
    layer_all = widen(out_cols.astype(jnp.bfloat16))
    qkv_all = widen(
        jnp.dot(normalize(layer_all, next_gain), w_qkv, preferred_element_type=jnp.float32).astype(
            jnp.bfloat16
        )
    )
    layer_rows = lax.dynamic_slice_in_dim(layer_all, fsdp_here * reqs, reqs, 0)
    qkv_rows = lax.dynamic_slice_in_dim(qkv_all, fsdp_here * reqs, reqs, 0)
    layer_width = width // seq_count
    qkv_width = 3 * width // seq_count
    layer_out = lax.dynamic_slice_in_dim(layer_rows, seq_here * layer_width, layer_width, 1)
    next_qkv = lax.dynamic_slice_in_dim(qkv_rows, seq_here * qkv_width, qkv_width, 1)
    return (packed_cache, block_summary, layer_out, next_qkv)


def solution(mesh):
    placed = (
        P(None, "fsdp", "seq", None),
        P("fsdp", "seq"),
        P("fsdp", "seq"),
        P("fsdp"),
        P("fsdp", None),
        P("fsdp", None),
        P(None, "fsdp"),
        P(None, "fsdp"),
        P(None, "fsdp"),
        P(None, "fsdp"),
        P(),
        P(),
    )
    return jax.shard_map(
        body,
        mesh=mesh,
        in_specs=placed,
        out_specs=(
            P(None, "fsdp", "seq", None),
            P(None, "fsdp", "seq", None),
            P("fsdp", "seq"),
            P("fsdp", "seq"),
        ),
        check_vma=False,
    )
```

profile of v0, /device:TPU:1, one launch (start us, length us, event | category | flops | bytes accessed | tf_op | source)
XLA Modules:
  0.0 290.0 jit_solution(1825323752103344393)
XLA Ops:
  2.8 1.3 dynamic-slice
  4.8 13.9 %all-reduce = s32[32]{0:T(128)S(1)} all-reduce(s32[32]{0:T(128)S(1)} %bitcast_dynamic-update-slice_fusion), channel_id=2, replica_groups=mesh['seq'=16,'fsdp'=16] {'seq'}, use_global_device_ids=true, to_apply=%add | all-reduce | flops 32 | bytes 256
  19.6 3.5 %all-to-all-start.1 = ((s32[1,16,2]{2,0,1:T(1,128)}), s32[1,16,2]{2,0,1:T(1,128)S(1)}, u32[]{:S(2)}, u32[]{:S(2)}) async-start(s32[1,16,2]{2,0,1:T(1,128)} %and_select_fusion), calls=%async_computation.1 | async-start | bytes 16384 | tf_op jit(solution)/shard_map/all_to_all | solution.py:118
  23.2 5.4 %fusion.7 = bf16[2,16,2,32,1280]{4,3,1,0,2:T(8,128)(2,1)S(1)} fusion(s32[2,16,32]{2,1,0:T(8,128)S(1)} %broadcast_add_fusion, s32[2,512]{1,0:T(2,128)S(1)} %broadcast_add_fusion.1, pred[2,512]{1,0:T(4,128)(4,1)S(1)} %get-tuple-element.236, bf16[2,2,512,1280]{3,2,1,0:T(8,128)(2,1)} %param.14), kind=kOutput, calls=%fused_computation.15 | convolution fusion | flops 2688024576 | bytes 10494976 | tf_op jit(solution)/shard_map/rtsp,crpd->ctrsd/dot_general | solution.py:113
  28.6 2.8 copy.45
  31.5 6.8 %all-to-all-start = ((bf16[2,16,2,32,1280]{4,3,0,2,1:T(8,128)(2,1)}), bf16[2,16,2,32,1280]{4,3,0,2,1:T(8,128)(2,1)}, u32[]{:S(2)}, u32[]{:S(2)}) async-start(bf16[2,16,2,32,1280]{4,3,0,2,1:T(8,128)(2,1)} %copy.45), calls=%async_computation | async-start | bytes 10485760 | tf_op jit(solution)/shard_map/all_to_all | solution.py:117
  38.8 4.8 %fusion.5 = f32[2,32,1,2,1280]{4,2,3,1,0:T(1,128)S(1)} fusion(f32[2,32,16,1,1]{2,3,4,1,0:T(1,128)S(1)} %bitcast.193, bf16[2,2,32,16,1280]{4,3,2,1,0:T(8,128)(2,1)} %bitcast.190), kind=kOutput, calls=%fused_computation.13 | convolution fusion | flops 31457280 | bytes 5902336 | tf_op jit(solution)/shard_map/rbk,crbkd->crbd/dot_general | solution.py:92
  45.6 24.9 %all-gather.2 = bf16[16,2,1280]{2,1,0:T(2,128)(2,1)S(1)} all-gather(bf16[1,2,1280]{2,1,0:T(2,128)(2,1)S(1)} %bitcast.202), channel_id=1, replica_groups=mesh['seq'=16,'fsdp'=16] {'fsdp'}, dimensions={0}, use_global_device_ids=true | all-gather | bytes 87040 | tf_op jit(solution)/shard_map/all_gather | solution.py:168
  73.7 30.8 %all-to-all-done = bf16[2,16,2,32,1280]{4,3,0,2,1:T(8,128)(2,1)} async-done(((bf16[2,16,2,32,1280]{4,3,0,2,1:T(8,128)(2,1)}), bf16[2,16,2,32,1280]{4,3,0,2,1:T(8,128)(2,1)}, u32[]{:S(2)}, u32[]{:S(2)}) %all-to-all-start) | async-done | bytes 5242912 | tf_op jit(solution)/shard_map/all_to_all | solution.py:117
  104.5 5.7 %fusion.12 = bf16[2,2,1280,512,1]{3,2,1,0,4:T(8,128)(2,1)S(1)} fusion(bf16[2,16,2,32,1280]{4,3,0,2,1:T(8,128)(2,1)} %all-to-all-done, s32[2,16,32]{2,0,1:T(2,128)S(1)} %iota_add_fusion, pred[2,16,32]{2,0,1:T(4,128)(4,1)S(1)} %iota_compare_fusion.1), kind=kOutput, calls=%fused_computation.19 | convolution fusion | flops 2685403136 | bytes 10490880 | tf_op jit(solution)/shard_map/rlts,ctrsd->crld/dot_general | solution.py:133
  110.9 1.9 copy-done.1
  115.4 7.9 %copy.55 = bf16[2,2,512,1280]{3,2,1,0:T(8,128)(2,1)} copy(bf16[2,2,512,1280]{2,3,1,0:T(8,128)(2,1)} %bitcast.188) | data formatting | bytes 10485760
  123.3 1.5 fusion.49
  125.7 18.9 %all-gather.1 = f32[32,16,80]{2,1,0:T(8,128)S(1)} all-gather(f32[2,16,80]{2,1,0:T(8,128)S(1)} %multiply_add_fusion), channel_id=3, replica_groups=mesh['seq'=16,'fsdp'=16] {'seq'}, dimensions={0}, use_global_device_ids=true | all-gather | bytes 174080 | tf_op jit(solution)/shard_map/all_gather | solution.py:13
  145.3 16.3 %all_gather.38 = f32[16,2,16]{2,1,0:T(2,128)S(1)} all-gather(f32[1,2,16]{2,1,0:T(2,128)S(1)} %get-tuple-element.239), channel_id=1, replica_groups=mesh['seq'=16,'fsdp'=16] {'seq'}, dimensions={0}, use_global_device_ids=true | all-gather | bytes 2176 | tf_op jit(solution)/shard_map/all_gather | solution.py:13
  161.6 16.5 %all_gather.37 = f32[16,2,16]{2,1,0:T(2,128)S(1)} all-gather(f32[1,2,16]{2,1,0:T(2,128)S(1)} %get-tuple-element.240), channel_id=1, replica_groups=mesh['seq'=16,'fsdp'=16] {'seq'}, dimensions={0}, use_global_device_ids=true | all-gather | bytes 2176 | tf_op jit(solution)/shard_map/all_gather | solution.py:13
  178.1 1.5 while.19
  180.5 41.5 %all-gather.3 = bf16[16,2,1280]{2,1,0:T(2,128)(2,1)S(1)} all-gather(bf16[1,2,1280]{2,1,0:T(2,128)(2,1)S(1)} %reshape.375), channel_id=1, replica_groups=mesh['seq'=16,'fsdp'=16] {'fsdp'}, dimensions={0}, use_global_device_ids=true | all-gather | bytes 87040 | tf_op jit(solution)/shard_map/all_gather | solution.py:167
  222.3 14.8 %all-gather.4 = bf16[16,80,32]{1,2,0:T(8,128)(2,1)S(1)} all-gather(bf16[1,80,32]{1,2,0:T(8,128)(2,1)S(1)} %fusion.21), channel_id=1, replica_groups=mesh['seq'=16,'fsdp'=16] {'fsdp'}, dimensions={0}, use_global_device_ids=true | all-gather | bytes 87040 | tf_op jit(solution)/shard_map/all_gather | solution.py:161
  237.4 1.2 fusion.57
  238.7 16.1 %all-gather.5 = bf16[16,80,32]{1,2,0:T(8,128)(2,1)S(1)} all-gather(bf16[1,80,32]{1,2,0:T(8,128)(2,1)S(1)} %fusion.57), channel_id=1, replica_groups=mesh['seq'=16,'fsdp'=16] {'fsdp'}, dimensions={0}, use_global_device_ids=true | all-gather | bytes 87040 | tf_op jit(solution)/shard_map/all_gather | solution.py:161
  255.0 1.1 fusion.20
  256.2 14.8 %all-gather.6 = bf16[16,80,32]{1,2,0:T(8,128)(2,1)S(1)} all-gather(bf16[1,80,32]{1,2,0:T(8,128)(2,1)S(1)} %fusion.20), channel_id=1, replica_groups=mesh['seq'=16,'fsdp'=16] {'fsdp'}, dimensions={0}, use_global_device_ids=true | all-gather | bytes 87040 | tf_op jit(solution)/shard_map/all_gather | solution.py:161
  271.6 16.6 %all-gather.7 = bf16[16,240,32]{1,2,0:T(8,128)(2,1)S(1)} all-gather(bf16[1,240,32]{1,2,0:T(8,128)(2,1)S(1)} %fusion.17), channel_id=1, replica_groups=mesh['seq'=16,'fsdp'=16] {'fsdp'}, dimensions={0}, use_global_device_ids=true | all-gather | bytes 261120 | tf_op jit(solution)/shard_map/all_gather | solution.py:161
  (136 shorter events, 19.2 us)
Async XLA Ops:
  0.6 270.7 %copy-start = (bf16[1280,240]{0,1:T(8,128)(2,1)S(1)}, bf16[1280,240]{0,1:T(8,128)(2,1)}, u32[]{:S(2)}) copy-start(bf16[1280,240]{0,1:T(8,128)(2,1)} %param.23) | copy-start | bytes 1843204
  19.6 11.9 %all-to-all-start.1 = ((s32[1,16,2]{2,0,1:T(1,128)}), s32[1,16,2]{2,0,1:T(1,128)S(1)}, u32[]{:S(2)}, u32[]{:S(2)}) async-start(s32[1,16,2]{2,0,1:T(1,128)} %and_select_fusion), calls=%async_computation.1 | async-start | bytes 16384 | tf_op jit(solution)/shard_map/all_to_all | solution.py:118
  31.5 6.8 %copy-start.10 = (f32[2,512]{1,0:T(2,128)S(1)}, f32[2,512]{1,0:T(2,128)}, u32[]{:S(2)}) copy-start(f32[2,512]{1,0:T(2,128)} %param.16) | copy-start | bytes 12292
  31.5 7.0 %copy-start.7 = (bf16[2,3840]{1,0:T(2,128)(2,1)S(1)}, bf16[2,3840]{1,0:T(2,128)(2,1)}, u32[]{:S(2)}) copy-start(bf16[2,3840]{1,0:T(2,128)(2,1)} %param.18) | copy-start | bytes 46084
  31.5 73.0 %all-to-all-start = ((bf16[2,16,2,32,1280]{4,3,0,2,1:T(8,128)(2,1)}), bf16[2,16,2,32,1280]{4,3,0,2,1:T(8,128)(2,1)}, u32[]{:S(2)}, u32[]{:S(2)}) async-start(bf16[2,16,2,32,1280]{4,3,0,2,1:T(8,128)(2,1)} %copy.45), calls=%async_computation | async-start | bytes 10485760 | tf_op jit(solution)/shard_map/all_to_all | solution.py:117
  38.3 7.3 %copy-start.9 = (bf16[2,1280]{1,0:T(2,128)(2,1)S(1)}, bf16[2,1280]{1,0:T(2,128)(2,1)}, u32[]{:S(2)}) copy-start(bf16[2,1280]{1,0:T(2,128)(2,1)} %param.19) | copy-start | bytes 15364
  43.7 0.7 copy-start.2
  71.6 38.6 %copy-start.4 = (f32[2,16]{1,0:T(2,128)}, f32[2,16]{1,0:T(2,128)S(1)}, u32[]{:S(2)}) copy-start(f32[2,16]{1,0:T(2,128)S(1)} %fusion.60) | copy-start | bytes 388
  110.5 2.3 copy-start.1
  110.5 3.5 %copy-start.5 = (f32[2,16]{1,0:T(2,128)S(1)}, f32[2,16]{1,0:T(2,128)}, u32[]{:S(2)}) copy-start(f32[2,16]{1,0:T(2,128)} %copy-done.4) | copy-start | bytes 388
  115.4 29.2 %copy-start.6 = (f32[2,16]{1,0:T(2,128)S(1)}, f32[2,16]{1,0:T(2,128)}, u32[]{:S(2)}) copy-start(f32[2,16]{1,0:T(2,128)} %copy-done.4) | copy-start | bytes 388
  115.4 106.6 %copy-start.3 = (bf16[1280,80]{0,1:T(8,128)(2,1)S(1)}, bf16[1280,80]{0,1:T(8,128)(2,1)}, u32[]{:S(2)}) copy-start(bf16[1280,80]{0,1:T(8,128)(2,1)} %param.20) | copy-start | bytes 614404
  123.3 148.0 %copy-start.8 = (f32[1280]{0:T(1024)S(1)}, f32[1280]{0:T(1024)}, u32[]{:S(2)}) copy-start(f32[1280]{0:T(1024)} %param.25) | copy-start | bytes 15364
where the time goes:
time: 291 us; the launch traced here: 290 us
  blocking collectives  194 us (67%)
  waiting for transfers between devices  30.8 us (11%)
  matrix products  21.6 us (7%)
  local copies, waits for them, and re-layouts  20.2 us (7%)
  other arithmetic  11 us (4%)
  starting transfers between devices  10.2 us (4%)
    all_gather x4, blocking collectives, widen(): return lax.all_gather(columns, 'fsdp', axis=1, tiled=True)  62.3 us
    all_gather x3, blocking collectives, combined_all(): gathered = jax.tree.map(lambda a: lax.all_gather(a, axis), part)  51.7 us
    all_gather x1, blocking collectives, body(): lax.all_gather(attended, 'fsdp', axis=0, tiled=True)  41.5 us
    all_to_all x1, waiting for transfers between devices, body(): lax.all_to_all(outgoing, 'seq', split_axis=1, concat_axis=1, tiled=True)  30.8 us
    all_gather x1, blocking collectives, body(): lax.all_gather(stream, 'fsdp', axis=0, tiled=True)  24.9 us
    unnamed x1, blocking collectives  13.9 us
    unnamed x35, local copies, waits for them, and re-layouts  13.1 us
    all_to_all x1, starting transfers between devices, body(): lax.all_to_all(outgoing, 'seq', split_axis=1, concat_axis=1, tiled=True)  6.77 us
  transfers between devices with their start and end apart: 2, of which 1 were waited for; matrix products, arithmetic and copies ran while one was open for 6% of the time, Pallas kernels for 0%

commit v1 on v0

--- a/solution.py
+++ b/solution.py
@@ -7,6 +7,19 @@
 H = 16
 BLK = 16
 neg_fill = -1e30
+
+
+def collect(shard, axis, dim):
+    ways = lax.axis_size(axis)
+    up = [(d, (d + 1) % ways) for d in range(ways)]
+    down = [(d, (d - 1) % ways) for d in range(ways)]
+    earlier, later = ([shard], [shard])
+    for _ in range(ways // 2):
+        earlier.append(lax.ppermute(earlier[-1], axis, up))
+    for _ in range((ways - 1) // 2):
+        later.append(lax.ppermute(later[-1], axis, down))
+    line = jnp.concatenate([*earlier[::-1], *later[1:]], axis=dim)
+    return jnp.roll(line, (lax.axis_index(axis) - ways // 2) * shard.shape[dim], axis=dim)
 
 
 def combined_all(part, axis, combine):
@@ -165,7 +178,7 @@
 
     attn_all, stream_all = (
         lax.all_gather(attended, "fsdp", axis=0, tiled=True),
-        lax.all_gather(stream, "fsdp", axis=0, tiled=True),
+        collect(stream, "fsdp", 0),
     )
     mid_cols = own_columns(stream_all, w_out.shape[1]).astype(jnp.float32) + jnp.dot(
         attn_all, w_out, preferred_element_type=jnp.float32

time: 291 us -> 287 us (0.986)
  starting transfers between devices: 10.2 us -> 35.2 us
  blocking collectives: 194 us -> 169 us
  local copies, waits for them, and re-layouts: 20.2 us -> 25.4 us
  other arithmetic: 11 us -> 5.92 us
  waiting for transfers between devices: 30.8 us -> 27.5 us
    all_gather x1 -> x0, blocking collectives: 24.9 us -> none  [body(): lax.all_gather(stream, 'fsdp', axis=0, tiled=True)]
    ppermute x0 -> x15, starting transfers between devices: none -> 24.9 us  [the longest x7 13.2 us: collect(): later.append(lax.ppermute(later[-1], axis, down))]
    all_to_all x1, waiting for transfers between devices: 30.8 us -> 18.4 us  [body(): lax.all_to_all(outgoing, 'seq', split_axis=1, concat_axis=1, tiled=True)]
    ppermute x0 -> x15, waiting for transfers between devices: none -> 9.06 us  [the longest x7 5.32 us: collect(): later.append(lax.ppermute(later[-1], axis, down))]
    concatenate x0 -> x1, local copies, waits for them, and re-layouts: none -> 5.15 us  [collect(): jnp.roll(line, (lax.axis_index(axis) - ways // 2) * shard.shape[dim], axi...]
    unnamed x35 -> x30, local copies, waits for them, and re-layouts: 13.1 us -> 13.1 us
  transfers between devices with their start and end apart: 2 -> 17, of which waited for: 1 -> 10; matrix products, arithmetic and copies ran while one was open for 6% -> 7% of each run, Pallas kernels for 0% -> 0%
where the time goes in v1:
time: 287 us; the launch traced here: 286 us
  blocking collectives  169 us (59%)
  starting transfers between devices  35.2 us (12%)
  waiting for transfers between devices  27.5 us (10%)
  local copies, waits for them, and re-layouts  25.4 us (9%)
  matrix products  21 us (7%)
  other arithmetic  5.92 us (2%)
    all_gather x4, blocking collectives, widen(): return lax.all_gather(columns, 'fsdp', axis=1, tiled=True)  62.3 us
    all_gather x3, blocking collectives, combined_all(): gathered = jax.tree.map(lambda a: lax.all_gather(a, axis), part)  51.9 us
    all_gather x1, blocking collectives, body(): lax.all_gather(attended, 'fsdp', axis=0, tiled=True)  41.4 us
    all_to_all x1, waiting for transfers between devices, body(): lax.all_to_all(outgoing, 'seq', split_axis=1, concat_axis=1, tiled=True)  18.4 us
    unnamed x1, blocking collectives  13.9 us
    ppermute x7, starting transfers between devices, collect(): later.append(lax.ppermute(later[-1], axis, down))  13.2 us
    unnamed x30, local copies, waits for them, and re-layouts  13.1 us
    ppermute x8, starting transfers between devices, collect(): earlier.append(lax.ppermute(earlier[-1], axis, up))  11.7 us
  transfers between devices with their start and end apart: 17, of which 10 were waited for; matrix products, arithmetic and copies ran while one was open for 7% of the time, Pallas kernels for 0%

profile of v1, /device:TPU:1, one launch (start us, length us, event | category | flops | bytes accessed | tf_op | source)
XLA Modules:
  0.0 286.1 jit_solution(15214044055958823088)
XLA Ops:
  4.8 13.9 %all-reduce = s32[32]{0:T(128)S(1)} all-reduce(s32[32]{0:T(128)S(1)} %bitcast_dynamic-update-slice_fusion), channel_id=2, replica_groups=mesh['seq'=16,'fsdp'=16] {'seq'}, use_global_device_ids=true, to_apply=%add | all-reduce | flops 32 | bytes 256
  19.6 3.5 %all-to-all-start.1 = ((s32[1,16,2]{2,0,1:T(1,128)}), s32[1,16,2]{2,0,1:T(1,128)S(1)}, u32[]{:S(2)}, u32[]{:S(2)}) async-start(s32[1,16,2]{2,0,1:T(1,128)} %and_select_fusion), calls=%async_computation.1 | async-start | bytes 16384 | tf_op jit(solution)/shard_map/all_to_all | solution.py:131
  23.2 5.4 %fusion.7 = bf16[2,16,2,32,1280]{4,3,1,0,2:T(8,128)(2,1)S(1)} fusion(s32[2,16,32]{2,1,0:T(8,128)S(1)} %broadcast_add_fusion, s32[2,512]{1,0:T(2,128)S(1)} %broadcast_add_fusion.1, pred[2,512]{1,0:T(4,128)(4,1)S(1)} %get-tuple-element.236, bf16[2,2,512,1280]{3,2,1,0:T(8,128)(2,1)} %param.14), kind=kOutput, calls=%fused_computation.15 | convolution fusion | flops 2688024576 | bytes 10494976 | tf_op jit(solution)/shard_map/rtsp,crpd->ctrsd/dot_general | solution.py:126
  28.6 2.8 copy.45
  31.5 6.8 %all-to-all-start = ((bf16[2,16,2,32,1280]{4,3,0,2,1:T(8,128)(2,1)}), bf16[2,16,2,32,1280]{4,3,0,2,1:T(8,128)(2,1)}, u32[]{:S(2)}, u32[]{:S(2)}) async-start(bf16[2,16,2,32,1280]{4,3,0,2,1:T(8,128)(2,1)} %copy.45), calls=%async_computation | async-start | bytes 10485760 | tf_op jit(solution)/shard_map/all_to_all | solution.py:130
  38.3 6.2 %collective-permute-start = (bf16[2,1280]{1,0:T(2,128)(2,1)S(1)}, bf16[2,1280]{1,0:T(2,128)(2,1)S(1)}, u32[]{:S(2)}, u32[]{:S(2)}) collective-permute-start(bf16[2,1280]{1,0:T(2,128)(2,1)S(1)} %copy-done.4), channel_id=1, source_target_pairs={{0,1},{1,2},{2,3},{3,4},{4,5},{5,6},{6,7},{7,8},{8,9},{9,10},{10,1... | collective-permute-start | bytes 15368 | tf_op jit(solution)/shard_map/ppermute | solution.py:18
  44.9 4.8 %fusion.5 = f32[2,32,1,2,1280]{4,2,3,1,0:T(1,128)S(1)} fusion(f32[2,32,16,1,1]{2,3,4,1,0:T(1,128)S(1)} %bitcast.192, bf16[2,2,32,16,1280]{4,3,2,1,0:T(8,128)(2,1)} %bitcast.189), kind=kOutput, calls=%fused_computation.13 | convolution fusion | flops 31457280 | bytes 5902336 | tf_op jit(solution)/shard_map/rbk,crbkd->crbd/dot_general | solution.py:105
  54.6 2.3 collective-permute-start.2
  64.6 3.1 %collective-permute-start.12 = (bf16[2,1280]{1,0:T(2,128)(2,1)S(1)}, bf16[2,1280]{1,0:T(2,128)(2,1)S(1)}, u32[]{:S(2)}, u32[]{:S(2)}) collective-permute-start(bf16[2,1280]{1,0:T(2,128)(2,1)S(1)} %collective-permute-done.11), channel_id=1, source_target_pairs={{0,15},{1,0},{2,1},{3,2},{4,3},{5,4},{6,5},{7,6},{8,7},{9,8},{10,9... | collective-permute-start | bytes 15368 | tf_op jit(solution)/shard_map/ppermute | solution.py:20
  68.5 3.8 %collective-permute-start.13 = (bf16[2,1280]{1,0:T(2,128)(2,1)S(1)}, bf16[2,1280]{1,0:T(2,128)(2,1)S(1)}, u32[]{:S(2)}, u32[]{:S(2)}) collective-permute-start(bf16[2,1280]{1,0:T(2,128)(2,1)S(1)} %collective-permute-done.12), channel_id=1, source_target_pairs={{0,15},{1,0},{2,1},{3,2},{4,3},{5,4},{6,5},{7,6},{8,7},{9,8},{10,9... | collective-permute-start | bytes 15368 | tf_op jit(solution)/shard_map/ppermute | solution.py:20
  73.1 3.8 %collective-permute-start.14 = (bf16[2,1280]{1,0:T(2,128)(2,1)S(1)}, bf16[2,1280]{1,0:T(2,128)(2,1)S(1)}, u32[]{:S(2)}, u32[]{:S(2)}) collective-permute-start(bf16[2,1280]{1,0:T(2,128)(2,1)S(1)} %collective-permute-done.13), channel_id=1, source_target_pairs={{0,15},{1,0},{2,1},{3,2},{4,3},{5,4},{6,5},{7,6},{8,7},{9,8},{10,9... | collective-permute-start | bytes 15368 | tf_op jit(solution)/shard_map/ppermute | solution.py:20
  77.8 3.2 %collective-permute-done.7 = bf16[2,1280]{1,0:T(2,128)(2,1)S(1)} collective-permute-done((bf16[2,1280]{1,0:T(2,128)(2,1)S(1)}, bf16[2,1280]{1,0:T(2,128)(2,1)S(1)}, u32[]{:S(2)}, u32[]{:S(2)}) %collective-permute-start.7) | collective-permute-done | bytes 5152 | tf_op jit(solution)/shard_map/ppermute | solution.py:18
  80.9 5.2 %concatenate.6 = bf16[64,1280]{1,0:T(8,128)(2,1)} concatenate(bf16[2,1280]{1,0:T(2,128)(2,1)S(1)} %collective-permute-done.7, bf16[2,1280]{1,0:T(2,128)(2,1)S(1)} %collective-permute-done.6, bf16[2,1280]{1,0:T(2,128)(2,1)S(1)} %collective-permute-done.5, bf16[2,1280]{1,0:T(2,128)(2,1)S(1)} %collective-permute-done.4, bf16[2,1280]{1,0:T(2,128)(2,1)S(1)} %collective-permute-done.3, ...), dimensions={0} | concatenate | bytes 327680 | tf_op jit(solution)/shard_map/jit(_roll_dynamic)/concatenate | solution.py:22
  86.1 18.4 %all-to-all-done = bf16[2,16,2,32,1280]{4,3,0,2,1:T(8,128)(2,1)} async-done(((bf16[2,16,2,32,1280]{4,3,0,2,1:T(8,128)(2,1)}), bf16[2,16,2,32,1280]{4,3,0,2,1:T(8,128)(2,1)}, u32[]{:S(2)}, u32[]{:S(2)}) %all-to-all-start) | async-done | bytes 5242912 | tf_op jit(solution)/shard_map/all_to_all | solution.py:130
  104.5 5.7 %fusion.12 = bf16[2,2,1280,512,1]{3,2,1,0,4:T(8,128)(2,1)S(1)} fusion(bf16[2,16,2,32,1280]{4,3,0,2,1:T(8,128)(2,1)} %all-to-all-done, s32[2,16,32]{2,0,1:T(2,128)S(1)} %iota_add_fusion, pred[2,16,32]{2,0,1:T(4,128)(4,1)S(1)} %iota_compare_fusion.1), kind=kOutput, calls=%fused_computation.19 | convolution fusion | flops 2685403136 | bytes 10490880 | tf_op jit(solution)/shard_map/rlts,ctrsd->crld/dot_general | solution.py:146
  113.7 7.9 %copy.55 = bf16[2,2,512,1280]{3,2,1,0:T(8,128)(2,1)} copy(bf16[2,2,512,1280]{2,3,1,0:T(8,128)(2,1)} %bitcast.187) | data formatting | bytes 10485760
  122.4 18.9 %all-gather.1 = f32[32,16,80]{2,1,0:T(8,128)S(1)} all-gather(f32[2,16,80]{2,1,0:T(8,128)S(1)} %multiply_add_fusion), channel_id=3, replica_groups=mesh['seq'=16,'fsdp'=16] {'seq'}, dimensions={0}, use_global_device_ids=true | all-gather | bytes 174080 | tf_op jit(solution)/shard_map/all_gather | solution.py:26
  141.4 16.3 %all_gather.34 = f32[16,2,16]{2,1,0:T(2,128)S(1)} all-gather(f32[1,2,16]{2,1,0:T(2,128)S(1)} %get-tuple-element.239), channel_id=1, replica_groups=mesh['seq'=16,'fsdp'=16] {'seq'}, dimensions={0}, use_global_device_ids=true | all-gather | bytes 2176 | tf_op jit(solution)/shard_map/all_gather | solution.py:26
  157.7 16.7 %all_gather.33 = f32[16,2,16]{2,1,0:T(2,128)S(1)} all-gather(f32[1,2,16]{2,1,0:T(2,128)S(1)} %get-tuple-element.240), channel_id=1, replica_groups=mesh['seq'=16,'fsdp'=16] {'seq'}, dimensions={0}, use_global_device_ids=true | all-gather | bytes 2176 | tf_op jit(solution)/shard_map/all_gather | solution.py:26
  176.1 41.4 %all-gather.2 = bf16[16,2,1280]{2,1,0:T(2,128)(2,1)S(1)} all-gather(bf16[1,2,1280]{2,1,0:T(2,128)(2,1)S(1)} %reshape.373), channel_id=1, replica_groups=mesh['seq'=16,'fsdp'=16] {'fsdp'}, dimensions={0}, use_global_device_ids=true | all-gather | bytes 87040 | tf_op jit(solution)/shard_map/all_gather | solution.py:180
  218.4 14.8 %all-gather.3 = bf16[16,80,32]{1,2,0:T(8,128)(2,1)S(1)} all-gather(bf16[1,80,32]{1,2,0:T(8,128)(2,1)S(1)} %fusion.59), channel_id=1, replica_groups=mesh['seq'=16,'fsdp'=16] {'fsdp'}, dimensions={0}, use_global_device_ids=true | all-gather | bytes 87040 | tf_op jit(solution)/shard_map/all_gather | solution.py:174
  234.8 16.1 %all-gather.4 = bf16[16,80,32]{1,2,0:T(8,128)(2,1)S(1)} all-gather(bf16[1,80,32]{1,2,0:T(8,128)(2,1)S(1)} %fusion.55), channel_id=1, replica_groups=mesh['seq'=16,'fsdp'=16] {'fsdp'}, dimensions={0}, use_global_device_ids=true | all-gather | bytes 87040 | tf_op jit(solution)/shard_map/all_gather | solution.py:174
  252.3 14.8 %all-gather.5 = bf16[16,80,32]{1,2,0:T(8,128)(2,1)S(1)} all-gather(bf16[1,80,32]{1,2,0:T(8,128)(2,1)S(1)} %fusion.19), channel_id=1, replica_groups=mesh['seq'=16,'fsdp'=16] {'fsdp'}, dimensions={0}, use_global_device_ids=true | all-gather | bytes 87040 | tf_op jit(solution)/shard_map/all_gather | solution.py:174
  267.8 16.5 %all-gather.6 = bf16[16,240,32]{1,2,0:T(8,128)(2,1)S(1)} all-gather(bf16[1,240,32]{1,2,0:T(8,128)(2,1)S(1)} %fusion.17), channel_id=1, replica_groups=mesh['seq'=16,'fsdp'=16] {'fsdp'}, dimensions={0}, use_global_device_ids=true | all-gather | bytes 261120 | tf_op jit(solution)/shard_map/all_gather | solution.py:174
  (161 shorter events, 33.6 us)
Async XLA Ops:
  0.6 266.9 %copy-start = (bf16[1280,240]{0,1:T(8,128)(2,1)S(1)}, bf16[1280,240]{0,1:T(8,128)(2,1)}, u32[]{:S(2)}) copy-start(bf16[1280,240]{0,1:T(8,128)(2,1)} %param.23) | copy-start | bytes 1843204
  19.6 11.9 %all-to-all-start.1 = ((s32[1,16,2]{2,0,1:T(1,128)}), s32[1,16,2]{2,0,1:T(1,128)S(1)}, u32[]{:S(2)}, u32[]{:S(2)}) async-start(s32[1,16,2]{2,0,1:T(1,128)} %and_select_fusion), calls=%async_computation.1 | async-start | bytes 16384 | tf_op jit(solution)/shard_map/all_to_all | solution.py:131
  31.5 6.8 %copy-start.4 = (bf16[2,1280]{1,0:T(2,128)(2,1)S(1)}, bf16[2,1280]{1,0:T(2,128)(2,1)}, u32[]{:S(2)}) copy-start(bf16[2,1280]{1,0:T(2,128)(2,1)} %param.19) | copy-start | bytes 15364
  31.5 13.1 %copy-start.7 = (f32[2,512]{1,0:T(2,128)S(1)}, f32[2,512]{1,0:T(2,128)}, u32[]{:S(2)}) copy-start(f32[2,512]{1,0:T(2,128)} %param.16) | copy-start | bytes 12292
  31.5 13.2 %copy-start.5 = (bf16[2,3840]{1,0:T(2,128)(2,1)S(1)}, bf16[2,3840]{1,0:T(2,128)(2,1)}, u32[]{:S(2)}) copy-start(bf16[2,3840]{1,0:T(2,128)(2,1)} %param.18) | copy-start | bytes 46084
  31.5 73.0 %all-to-all-start = ((bf16[2,16,2,32,1280]{4,3,0,2,1:T(8,128)(2,1)}), bf16[2,16,2,32,1280]{4,3,0,2,1:T(8,128)(2,1)}, u32[]{:S(2)}, u32[]{:S(2)}) async-start(bf16[2,16,2,32,1280]{4,3,0,2,1:T(8,128)(2,1)} %copy.45), calls=%async_computation | async-start | bytes 10485760 | tf_op jit(solution)/shard_map/all_to_all | solution.py:130
  38.3 13.8 %collective-permute-start = (bf16[2,1280]{1,0:T(2,128)(2,1)S(1)}, bf16[2,1280]{1,0:T(2,128)(2,1)S(1)}, u32[]{:S(2)}, u32[]{:S(2)}) collective-permute-start(bf16[2,1280]{1,0:T(2,128)(2,1)S(1)} %copy-done.4), channel_id=1, source_target_pairs={{0,1},{1,2},{2,3},{3,4},{4,5},{5,6},{6,7},{7,8},{8,9},{9,10},{10,1... | collective-permute-start | bytes 15368 | tf_op jit(solution)/shard_map/ppermute | solution.py:18
  44.5 9.7 %collective-permute-start.8 = (bf16[2,1280]{1,0:T(2,128)(2,1)S(1)}, bf16[2,1280]{1,0:T(2,128)(2,1)S(1)}, u32[]{:S(2)}, u32[]{:S(2)}) collective-permute-start(bf16[2,1280]{1,0:T(2,128)(2,1)S(1)} %copy-done.4), channel_id=1, source_target_pairs={{0,15},{1,0},{2,1},{3,2},{4,3},{5,4},{6,5},{7,6},{8,7},{9,8},{10,9... | collective-permute-start | bytes 15368 | tf_op jit(solution)/shard_map/ppermute | solution.py:20
  52.1 2.5 collective-permute-start.1
  54.2 3.5 %collective-permute-start.9 = (bf16[2,1280]{1,0:T(2,128)(2,1)S(1)}, bf16[2,1280]{1,0:T(2,128)(2,1)S(1)}, u32[]{:S(2)}, u32[]{:S(2)}) collective-permute-start(bf16[2,1280]{1,0:T(2,128)(2,1)S(1)} %collective-permute-done.8), channel_id=1, source_target_pairs={{0,15},{1,0},{2,1},{3,2},{4,3},{5,4},{6,5},{7,6},{8,7},{9,8},{10,9... | collective-permute-start | bytes 15368 | tf_op jit(solution)/shard_map/ppermute | solution.py:20
  54.6 3.9 %collective-permute-start.2 = (bf16[2,1280]{1,0:T(2,128)(2,1)S(1)}, bf16[2,1280]{1,0:T(2,128)(2,1)S(1)}, u32[]{:S(2)}, u32[]{:S(2)}) collective-permute-start(bf16[2,1280]{1,0:T(2,128)(2,1)S(1)} %collective-permute-done.1), channel_id=1, source_target_pairs={{0,1},{1,2},{2,3},{3,4},{4,5},{5,6},{6,7},{7,8},{8,9},{9,10},{10,1... | collective-permute-start | bytes 15368 | tf_op jit(solution)/shard_map/ppermute | solution.py:18
  57.7 3.4 %collective-permute-start.10 = (bf16[2,1280]{1,0:T(2,128)(2,1)S(1)}, bf16[2,1280]{1,0:T(2,128)(2,1)S(1)}, u32[]{:S(2)}, u32[]{:S(2)}) collective-permute-start(bf16[2,1280]{1,0:T(2,128)(2,1)S(1)} %collective-permute-done.9), channel_id=1, source_target_pairs={{0,15},{1,0},{2,1},{3,2},{4,3},{5,4},{6,5},{7,6},{8,7},{9,8},{10,9... | collective-permute-start | bytes 15368 | tf_op jit(solution)/shard_map/ppermute | solution.py:20
  58.5 4.4 %collective-permute-start.3 = (bf16[2,1280]{1,0:T(2,128)(2,1)S(1)}, bf16[2,1280]{1,0:T(2,128)(2,1)S(1)}, u32[]{:S(2)}, u32[]{:S(2)}) collective-permute-start(bf16[2,1280]{1,0:T(2,128)(2,1)S(1)} %collective-permute-done.2), channel_id=1, source_target_pairs={{0,1},{1,2},{2,3},{3,4},{4,5},{5,6},{6,7},{7,8},{8,9},{9,10},{10,1... | collective-permute-start | bytes 15368 | tf_op jit(solution)/shard_map/ppermute | solution.py:18
  61.1 3.4 %collective-permute-start.11 = (bf16[2,1280]{1,0:T(2,128)(2,1)S(1)}, bf16[2,1280]{1,0:T(2,128)(2,1)S(1)}, u32[]{:S(2)}, u32[]{:S(2)}) collective-permute-start(bf16[2,1280]{1,0:T(2,128)(2,1)S(1)} %collective-permute-done.10), channel_id=1, source_target_pairs={{0,15},{1,0},{2,1},{3,2},{4,3},{5,4},{6,5},{7,6},{8,7},{9,8},{10,9... | collective-permute-start | bytes 15368 | tf_op jit(solution)/shard_map/ppermute | solution.py:20
  63.0 4.7 %collective-permute-start.4 = (bf16[2,1280]{1,0:T(2,128)(2,1)S(1)}, bf16[2,1280]{1,0:T(2,128)(2,1)S(1)}, u32[]{:S(2)}, u32[]{:S(2)}) collective-permute-start(bf16[2,1280]{1,0:T(2,128)(2,1)S(1)} %collective-permute-done.3), channel_id=1, source_target_pairs={{0,1},{1,2},{2,3},{3,4},{4,5},{5,6},{6,7},{7,8},{8,9},{9,10},{10,1... | collective-permute-start | bytes 15368 | tf_op jit(solution)/shard_map/ppermute | solution.py:18
  64.6 3.9 %collective-permute-start.12 = (bf16[2,1280]{1,0:T(2,128)(2,1)S(1)}, bf16[2,1280]{1,0:T(2,128)(2,1)S(1)}, u32[]{:S(2)}, u32[]{:S(2)}) collective-permute-start(bf16[2,1280]{1,0:T(2,128)(2,1)S(1)} %collective-permute-done.11), channel_id=1, source_target_pairs={{0,15},{1,0},{2,1},{3,2},{4,3},{5,4},{6,5},{7,6},{8,7},{9,8},{10,9... | collective-permute-start | bytes 15368 | tf_op jit(solution)/shard_map/ppermute | solution.py:20
  67.6 4.7 %collective-permute-start.5 = (bf16[2,1280]{1,0:T(2,128)(2,1)S(1)}, bf16[2,1280]{1,0:T(2,128)(2,1)S(1)}, u32[]{:S(2)}, u32[]{:S(2)}) collective-permute-start(bf16[2,1280]{1,0:T(2,128)(2,1)S(1)} %collective-permute-done.4), channel_id=1, source_target_pairs={{0,1},{1,2},{2,3},{3,4},{4,5},{5,6},{6,7},{7,8},{8,9},{9,10},{10,1... | collective-permute-start | bytes 15368 | tf_op jit(solution)/shard_map/ppermute | solution.py:18
  68.5 4.7 %collective-permute-start.13 = (bf16[2,1280]{1,0:T(2,128)(2,1)S(1)}, bf16[2,1280]{1,0:T(2,128)(2,1)S(1)}, u32[]{:S(2)}, u32[]{:S(2)}) collective-permute-start(bf16[2,1280]{1,0:T(2,128)(2,1)S(1)} %collective-permute-done.12), channel_id=1, source_target_pairs={{0,15},{1,0},{2,1},{3,2},{4,3},{5,4},{6,5},{7,6},{8,7},{9,8},{10,9... | collective-permute-start | bytes 15368 | tf_op jit(solution)/shard_map/ppermute | solution.py:20
  72.3 4.7 %collective-permute-start.6 = (bf16[2,1280]{1,0:T(2,128)(2,1)S(1)}, bf16[2,1280]{1,0:T(2,128)(2,1)S(1)}, u32[]{:S(2)}, u32[]{:S(2)}) collective-permute-start(bf16[2,1280]{1,0:T(2,128)(2,1)S(1)} %collective-permute-done.5), channel_id=1, source_target_pairs={{0,1},{1,2},{2,3},{3,4},{4,5},{5,6},{6,7},{7,8},{8,9},{9,10},{10,1... | collective-permute-start | bytes 15368 | tf_op jit(solution)/shard_map/ppermute | solution.py:18
  73.1 4.7 %collective-permute-start.14 = (bf16[2,1280]{1,0:T(2,128)(2,1)S(1)}, bf16[2,1280]{1,0:T(2,128)(2,1)S(1)}, u32[]{:S(2)}, u32[]{:S(2)}) collective-permute-start(bf16[2,1280]{1,0:T(2,128)(2,1)S(1)} %collective-permute-done.13), channel_id=1, source_target_pairs={{0,15},{1,0},{2,1},{3,2},{4,3},{5,4},{6,5},{7,6},{8,7},{9,8},{10,9... | collective-permute-start | bytes 15368 | tf_op jit(solution)/shard_map/ppermute | solution.py:20
  77.0 4.0 %collective-permute-start.7 = (bf16[2,1280]{1,0:T(2,128)(2,1)S(1)}, bf16[2,1280]{1,0:T(2,128)(2,1)S(1)}, u32[]{:S(2)}, u32[]{:S(2)}) collective-permute-start(bf16[2,1280]{1,0:T(2,128)(2,1)S(1)} %collective-permute-done.6), channel_id=1, source_target_pairs={{0,1},{1,2},{2,3},{3,4},{4,5},{5,6},{6,7},{7,8},{8,9},{9,10},{10,1... | collective-permute-start | bytes 15368 | tf_op jit(solution)/shard_map/ppermute | solution.py:18
  113.7 103.8 %copy-start.3 = (bf16[1280,80]{0,1:T(8,128)(2,1)S(1)}, bf16[1280,80]{0,1:T(8,128)(2,1)}, u32[]{:S(2)}) copy-start(bf16[1280,80]{0,1:T(8,128)(2,1)} %param.20) | copy-start | bytes 614404
  113.7 119.9 %copy-start.8 = (f32[1280]{0:T(1024)S(1)}, f32[1280]{0:T(1024)}, u32[]{:S(2)}) copy-start(f32[1280]{0:T(1024)} %param.24) | copy-start | bytes 15364
  121.6 145.9 %copy-start.6 = (f32[1280]{0:T(1024)S(1)}, f32[1280]{0:T(1024)}, u32[]{:S(2)}) copy-start(f32[1280]{0:T(1024)} %param.25) | copy-start | bytes 15364
  (2 other events, 3.0 us)
